TPU v7x, 256 devices: a whole 4x4x8 slice. The times are simulated.
256 devices in a mesh: gene: 4 (over z_hi), cell: 64 (over x, y, z_lo, core).
Axes of the slice: x: 4, y: 4, z: 8 (z_hi: 4, z_lo: 2; z = z_hi * 2 + z_lo), core: 2. Of those that a mesh axis runs over, the one named last changes fastest.
Arguments:
- counts: int32 [16384, 32768], P('gene', 'cell'), may hold values from 0 to 2047, as said below
- w1: bfloat16 [16384, 512], P(('gene', 'cell')), may hold values from 0.099609375 to 2
- h1: float32 [512, 32768], P(None, 'cell'), may hold values from 0.1 to 2
- w2: float32 [512, 64], replicated, may hold values from 0.1 to 2
- h2: float32 [64, 32768], P(None, 'cell'), may hold values from 0.005 to 0.1
Outputs:
- w1_new: bfloat16 [16384, 512], P(('gene', 'cell'))
- h1_new: float32 [512, 32768], P(None, 'cell')
- w2_new: float32 [512, 64], replicated
- h2_new: float32 [64, 32768], P(None, 'cell')
Inputs may be any that keep to these rules, and one draw needn't show every extreme that they name: `counts`: counts are whole numbers; a gene's and a cell's typical depth vary, and cells later in the order run deeper.
All inputs are finite; a program needn't handle non-finite values.
Results may differ from a plain program's by a relative error of at most 0.0013.
The roundings to bfloat16 on the way count: a program that leaves them out, or rounds other values in their place, can miss the bound.
Values may be sent and summed in bfloat16 or wider, within the bound.
A program may use at most 64 MiB of HBM per device.

v0:
```python
import jax
import jax.numpy as jnp
from jax import lax
from jax.sharding import PartitionSpec as P


def layer_two(h1_new, w2, h2):
    hi = lax.Precision.HIGHEST
    ratio3 = h1_new / jnp.dot(w2, h2, precision=hi)
    h2_new = h2 * jnp.dot(w2.T, ratio3, precision=hi) / jnp.sum(w2, axis=0)[:, None]
    ratio4 = h1_new / jnp.dot(w2, h2_new, precision=hi)
    w2_part = jnp.dot(ratio4, h2_new.T, precision=hi)
    h2_part = jnp.sum(h2_new, axis=1)
    return (h2_new, w2_part, h2_part)


def on_device(counts, w1, h1, w2, h2):
    w1_block = lax.all_gather(w1, "cell", axis=0, tiled=True)
    values = counts.astype(jnp.float32)
    h1_low = h1.astype(jnp.bfloat16)
    approx = jnp.dot(w1_block, h1_low, preferred_element_type=jnp.float32)
    ratio = (values / approx).astype(jnp.bfloat16)
    partial_num = lax.dot_general(
        w1_block, ratio, (((0,), (0,)), ((), ())), preferred_element_type=jnp.float32
    )
    partial_col = jnp.sum(w1_block.astype(jnp.float32), axis=0)
    h1_num, colsum = lax.psum((partial_num, partial_col), "gene")
    h1_new = h1 * h1_num / colsum[:, None]
    h1_low2 = h1_new.astype(jnp.bfloat16)
    approx2 = jnp.dot(w1_block, h1_low2, preferred_element_type=jnp.float32)
    ratio2 = (values / approx2).astype(jnp.bfloat16)
    local_rows = jnp.sum(h1_new, axis=1)
    rowsum = lax.psum(local_rows, "cell")
    w1_num = lax.psum_scatter(
        lax.dot_general(
            ratio2, h1_low2, (((1,), (1,)), ((), ())), preferred_element_type=jnp.float32
        ),
        "cell",
        scatter_dimension=0,
        tiled=True,
    )
    w1_new = (w1.astype(jnp.float32) * w1_num / rowsum[None, :]).astype(jnp.bfloat16)
    h2_new, w2_part, h2_part = layer_two(h1_new, w2, h2)
    w2_num, h2_rows = lax.psum((w2_part, h2_part), "cell")
    w2_new = w2 * w2_num / h2_rows[None, :]
    return (w1_new, h1_new, w2_new, h2_new)


def solution(mesh):
    placed = (P("gene", "cell"), P(("gene", "cell"), None), P(None, "cell"), P(), P(None, "cell"))
    return jax.shard_map(
        on_device,
        mesh=mesh,
        in_specs=placed,
        out_specs=(P(("gene", "cell"), None), P(None, "cell"), P(), P(None, "cell")),
        check_vma=False,
    )
```

profile of v0, /device:TPU:64, one launch (start us, length us, event | category | flops | bytes accessed | tf_op | source)
XLA Modules:
  0.0 999.0 jit_solution(18031313151263550134)
XLA Ops:
  7.2 0.0 all-gather.2.cloned.1.call-start
  7.2 0.7 all-gather.2.cloned.1.call-update
  7.9 0.0 copy-start.1
  7.9 0.0 copy-start
  7.9 0.0 all-reduce.4.cloned.1.call-start
  8.0 112.6 %all-gather.2.cloned.1.call-done = bf16[4096,512]{1,0:T(8,128)(2,1)} async-done(((bf16[64,512]{1,0:T(8,128)(2,1)}), bf16[4096,512]{1,0:T(8,128)(2,1)}) %all-gather.2.cloned.1.call-update) | async-done | bytes 4194320 | tf_op jit(solution)/shard_map/all_gather | solution.py:18
  120.6 11.9 %fusion.8 = f32[512,512]{0,1:T(8,128)} fusion(bf16[4096,512]{1,0:T(8,128)(2,1)} %all-gather.2.cloned.1.call-done, s32[4096,512]{1,0:T(8,128)} %param.5, f32[512,512]{1,0:T(8,128)} %param.7), kind=kOutput, calls=%fused_computation.12 | convolution fusion | flops 4301520896 | bytes 14680064 | tf_op jit(solution)/shard_map/dot_general | solution.py:23
  132.5 0.0 copy-start.5
  132.5 0.0 all-reduce.4.cloned.1.call-update
  132.6 0.0 all-reduce.6.cloned.1.call-start
  132.6 0.0 copy-done.1
  132.6 0.3 copy.9
  133.0 0.0 copy-done
  133.0 0.1 reduce_sum.38
  133.1 2.8 convert_reduce_fusion
  135.9 11.2 %psum.36 = f32[512]{0:T(512)S(1)} all-reduce(f32[512]{0:T(512)S(1)} %convert_reduce_fusion), channel_id=1, replica_groups=mesh['gene'=4,'cell'=64] {'gene'}, use_global_device_ids=true, to_apply=%region_2.0 | all-reduce | flops 512 | bytes 4096 | tf_op jit(solution)/shard_map/psum | solution.py:27
  147.1 50.6 %all-reduce.4.cloned.1.call-done = f32[512,512]{0,1:T(8,128)} async-done(((f32[512,512]{0,1:T(8,128)}), f32[512,512]{0,1:T(8,128)}) %all-reduce.4.cloned.1.call-update) | async-done | bytes 1048592 | tf_op jit(solution)/shard_map/psum | solution.py:27
  197.7 0.0 copy-done.5
  197.7 0.0 copy-start.2
  197.7 2.5 fusion.6
  200.2 1.2 fusion.16
  201.4 0.0 copy-start.3
  201.4 0.0 copy-done.2
  201.4 1.2 fusion.7
  202.6 1.5 fusion.17
  204.1 0.0 all-reduce.6.cloned.1.call-update
  204.1 0.2 reduce-scatter.2.cloned.1.call-start
  204.3 0.3 fusion.15
  204.6 0.0 copy-done.3
  204.6 12.5 %fusion.4 = f32[4096,512]{1,0:T(8,128)} fusion(s32[4096,512]{1,0:T(8,128)} %param.5, bf16[4096,512]{1,0:T(8,128)(2,1)} %all-gather.2.cloned.1.call-done, f32[512,512]{0,1:T(8,128)S(1)} %get-tuple-element.11), kind=kOutput, calls=%fused_computation.6 | convolution fusion | flops 4301783040 | bytes 22020096 | tf_op jit(solution)/shard_map/dot_general | solution.py:35
  217.1 0.0 copy-start.4
  217.1 0.0 reduce-scatter.2.cloned.1.call-update
  217.1 1.3 copy.10
  218.4 142.9 %all-reduce = (f32[512]{0:T(512)S(1)}, f32[64]{0:T(128)S(1)}) all-reduce(f32[512]{0:T(512)S(1)} %get-tuple-element.10, f32[64]{0:T(128)S(1)} %get-tuple-element.12), channel_id=1, replica_groups=mesh['gene'=4,'cell'=64] {'cell'}, use_global_device_ids=true, to_apply=%region_5.0 | all-reduce | flops 576 | bytes 4608 | tf_op jit(solution)/shard_map/psum | solution.py:33
  361.3 328.9 %all-reduce.6.cloned.1.call-done = f32[512,64]{0,1:T(8,128)} async-done(((f32[512,64]{0,1:T(8,128)}), f32[512,64]{0,1:T(8,128)}) %all-reduce.6.cloned.1.call-update) | async-done | bytes 131088 | tf_op jit(solution)/shard_map/psum | solution.py:44
  690.2 1.6 multiply_divide_fusion
  691.9 299.1 %reduce-scatter.2.cloned.1.call-done = f32[64,512]{1,0:T(8,128)} async-done(((f32[4096,512]{1,0:T(8,128)}), f32[64,512]{1,0:T(8,128)}) %reduce-scatter.2.cloned.1.call-update) | async-done | bytes 131088 | tf_op jit(solution)/shard_map/reduce_scatter | solution.py:34
  990.9 0.0 copy-done.4
  990.9 1.6 divide_convert_fusion.4
Async XLA Ops:
  7.2 113.4 %all-gather.2.cloned.1.call-start = ((), (), s32[]{:S(2)}) async-start(), calls=%async_computation.1 | async-start | bytes 4259840 | tf_op jit(solution)/shard_map/all_gather | solution.py:18
  7.9 124.7 %copy-start.1 = (f32[512,512]{1,0:T(8,128)S(1)}, f32[512,512]{1,0:T(8,128)}, u32[]{:S(2)}) copy-start(f32[512,512]{1,0:T(8,128)} %param.7) | copy-start | bytes 3145732
  7.9 125.1 %copy-start = (f32[512,64]{0,1:T(8,128)S(1)}, f32[512,64]{0,1:T(8,128)}, u32[]{:S(2)}) copy-start(f32[512,64]{0,1:T(8,128)} %param.8) | copy-start | bytes 393220
  7.9 189.8 %all-reduce.4.cloned.1.call-start = ((), (), s32[]{:S(2)}) async-start(), calls=%async_computation.2 | async-start | bytes 2097152 | tf_op jit(solution)/shard_map/psum | solution.py:27
  132.5 65.2 %copy-start.5 = (f32[64,512]{1,0:T(8,128)S(1)}, f32[64,512]{1,0:T(8,128)}, u32[]{:S(2)}) copy-start(f32[64,512]{1,0:T(8,128)} %param.9) | copy-start | bytes 393220
  132.6 557.7 %all-reduce.6.cloned.1.call-start = ((), (), s32[]{:S(2)}) async-start(), calls=%async_computation.4 | async-start | bytes 262144 | tf_op jit(solution)/shard_map/psum | solution.py:44
  197.7 3.7 copy-start.2
  201.4 3.2 copy-start.3
  204.1 786.8 %reduce-scatter.2.cloned.1.call-start = ((), (), s32[]{:S(2)}) async-start(), calls=%async_computation.3 | async-start | bytes 8519680 | tf_op jit(solution)/shard_map/reduce_scatter | solution.py:34
  217.1 773.8 %copy-start.4 = (bf16[64,512]{1,0:T(8,128)(2,1)S(1)}, bf16[64,512]{1,0:T(8,128)(2,1)}, u32[]{:S(2)}) copy-start(bf16[64,512]{1,0:T(8,128)(2,1)} %param.6) | copy-start | bytes 196612
Sparse Core Ops, SparseCore 0:
  9.9 110.7 all-gather.1
  132.7 64.9 all-reduce.3
  204.2 485.9 all-reduce.5
  692.6 298.2 reduce-scatter.1
where the time goes:
time: 999 us
  waiting for transfers between devices  792 us (79%)
  blocking collectives  154 us (15%)
  matrix products  30.7 us (3%)
  between operations  13.8 us (1%)
    psum x1, waiting for transfers between devices, on_device(): w2_num, h2_rows = lax.psum((w2_part, h2_part), 'cell')  329 us
    reduce_scatter x1, waiting for transfers between devices, on_device(): lax.psum_scatter(lax.dot_general(ratio2, h1_low2, (((1,), (1,)), ((), ())...  299 us
    psum x1, blocking collectives, on_device(): rowsum = lax.psum(local_rows, 'cell')  143 us
    all_gather x1, waiting for transfers between devices, on_device(): w1_block = lax.all_gather(w1, 'cell', axis=0, tiled=True)  113 us
    psum x1, waiting for transfers between devices, on_device(): h1_num, colsum = lax.psum((partial_num, partial_col), 'gene')  50.6 us
  transfers between devices with their start and end apart: 4, of which 4 were waited for; matrix products, arithmetic and copies ran while one was open for 2% of the time, Pallas kernels for 0%

commit v1 on v0

--- a/solution.py
+++ b/solution.py
@@ -2,6 +2,13 @@
 import jax.numpy as jnp
 from jax import lax
 from jax.sharding import PartitionSpec as P
+
+
+def _view_windows(xx):
+    passed = jnp.stack([xx for _ in range(lax.axis_size("cell"))], axis=0)
+    piece_out = lax.all_to_all(passed, axis_name="cell", split_axis=0, concat_axis=0)
+    row_out = jnp.concatenate(piece_out, 0)
+    return row_out
 
 
 def layer_two(h1_new, w2, h2):
@@ -15,7 +22,7 @@
 
 
 def on_device(counts, w1, h1, w2, h2):
-    w1_block = lax.all_gather(w1, "cell", axis=0, tiled=True)
+    w1_block = _view_windows(w1)
     values = counts.astype(jnp.float32)
     h1_low = h1.astype(jnp.bfloat16)
     approx = jnp.dot(w1_block, h1_low, preferred_element_type=jnp.float32)

time: 999 us -> 949 us (0.950)
  waiting for transfers between devices: 792 us -> 679 us
  blocking collectives: 154 us -> 215 us
    all_gather x1 -> x0, waiting for transfers between devices: 113 us -> none  [on_device(): w1_block = lax.all_gather(w1, 'cell', axis=0, tiled=True)]
    all_to_all x0 -> x1, blocking collectives: none -> 61.2 us  [_view_windows(): lax.all_to_all(passed, axis_name='cell', split_axis=0, concat_axis=0)]
  transfers between devices with their start and end apart: 4 -> 3, of which waited for: 4 -> 3; matrix products, arithmetic and copies ran while one was open for 2% -> 2% of each run, Pallas kernels for 0% -> 0%
where the time goes in v1:
time: 949 us; the launch traced here: 948 us
  waiting for transfers between devices  679 us (72%)
  blocking collectives  215 us (23%)
  matrix products  30.4 us (3%)
  between operations  13.8 us (1%)
    psum x1, waiting for transfers between devices, on_device(): w2_num, h2_rows = lax.psum((w2_part, h2_part), 'cell')  329 us
    reduce_scatter x1, waiting for transfers between devices, on_device(): lax.psum_scatter(lax.dot_general(ratio2, h1_low2, (((1,), (1,)), ((), ())...  299 us
    psum x1, blocking collectives, on_device(): rowsum = lax.psum(local_rows, 'cell')  143 us
    all_to_all x1, blocking collectives, _view_windows(): lax.all_to_all(passed, axis_name='cell', split_axis=0, concat_axis=0)  61.2 us
    psum x1, waiting for transfers between devices, on_device(): h1_num, colsum = lax.psum((partial_num, partial_col), 'gene')  50.7 us
  transfers between devices with their start and end apart: 3, of which 3 were waited for; matrix products, arithmetic and copies ran while one was open for 2% of the time, Pallas kernels for 0%

profile of v1, /device:TPU:64, one launch (start us, length us, event | category | flops | bytes accessed | tf_op | source)
XLA Modules:
  0.0 948.2 jit_solution(10383549977356017198)
XLA Ops:
  7.2 0.0 all-reduce.4.cloned.1.call-start
  7.2 1.3 stack.2
  8.6 0.0 copy-start.1
  8.6 61.2 %all_to_all.5 = bf16[64,64,512]{2,1,0:T(8,128)(2,1)} all-to-all(bf16[64,64,512]{2,1,0:T(8,128)(2,1)S(1)} %stack.2), channel_id=1, replica_groups=mesh['gene'=4,'cell'=64] {'cell'}, dimensions={0} | all-to-all | bytes 8388608 | tf_op jit(solution)/shard_map/all_to_all | solution.py:9
  69.8 0.0 copy-done.1
  69.8 0.0 copy-start
  69.8 11.6 %fusion.8 = f32[512,512]{0,1:T(8,128)} fusion(bf16[4096,512]{1,0:T(8,128)(2,1)} %bitcast.30, s32[4096,512]{1,0:T(8,128)} %param.5, f32[512,512]{1,0:T(8,128)S(1)} %copy-done.1), kind=kOutput, calls=%fused_computation.12 | convolution fusion | flops 4301520896 | bytes 14680064 | tf_op jit(solution)/shard_map/dot_general | solution.py:30
  81.3 0.0 copy-start.5
  81.3 0.0 all-reduce.4.cloned.1.call-update
  81.4 0.0 all-reduce.6.cloned.1.call-start
  81.4 0.3 copy.11
  81.8 0.0 copy-done
  81.8 0.1 reduce_sum.38
  81.9 2.8 convert_reduce_fusion
  84.7 11.4 %psum.36 = f32[512]{0:T(512)S(1)} all-reduce(f32[512]{0:T(512)S(1)} %convert_reduce_fusion), channel_id=1, replica_groups=mesh['gene'=4,'cell'=64] {'gene'}, use_global_device_ids=true, to_apply=%region_2.0 | all-reduce | flops 512 | bytes 4096 | tf_op jit(solution)/shard_map/psum | solution.py:34
  96.1 50.7 %all-reduce.4.cloned.1.call-done = f32[512,512]{0,1:T(8,128)} async-done(((f32[512,512]{0,1:T(8,128)}), f32[512,512]{0,1:T(8,128)}) %all-reduce.4.cloned.1.call-update) | async-done | bytes 1048592 | tf_op jit(solution)/shard_map/psum | solution.py:34
  146.8 0.0 copy-done.5
  146.8 0.0 copy-start.2
  146.8 2.5 fusion.6
  149.3 1.2 fusion.16
  150.5 0.0 copy-start.3
  150.5 0.0 copy-done.2
  150.5 1.2 fusion.7
  151.7 1.5 fusion.17
  153.1 0.0 all-reduce.6.cloned.1.call-update
  153.2 0.2 reduce-scatter.2.cloned.1.call-start
  153.4 0.3 fusion.15
  153.7 0.0 copy-done.3
  153.7 12.5 %fusion.4 = f32[4096,512]{1,0:T(8,128)} fusion(s32[4096,512]{1,0:T(8,128)} %param.5, bf16[4096,512]{1,0:T(8,128)(2,1)} %bitcast.31, f32[512,512]{0,1:T(8,128)S(1)} %get-tuple-element.15), kind=kOutput, calls=%fused_computation.6 | convolution fusion | flops 4301783040 | bytes 22020096 | tf_op jit(solution)/shard_map/dot_general | solution.py:42
  166.2 0.0 copy-start.4
  166.2 0.0 reduce-scatter.2.cloned.1.call-update
  166.2 1.3 copy.12
  167.5 142.9 %all-reduce = (f32[512]{0:T(512)S(1)}, f32[64]{0:T(128)S(1)}) all-reduce(f32[512]{0:T(512)S(1)} %get-tuple-element.14, f32[64]{0:T(128)S(1)} %get-tuple-element.16), channel_id=1, replica_groups=mesh['gene'=4,'cell'=64] {'cell'}, use_global_device_ids=true, to_apply=%region_5.0 | all-reduce | flops 576 | bytes 4608 | tf_op jit(solution)/shard_map/psum | solution.py:40
  310.4 328.9 %all-reduce.6.cloned.1.call-done = f32[512,64]{0,1:T(8,128)} async-done(((f32[512,64]{0,1:T(8,128)}), f32[512,64]{0,1:T(8,128)}) %all-reduce.6.cloned.1.call-update) | async-done | bytes 131088 | tf_op jit(solution)/shard_map/psum | solution.py:51
  639.3 1.6 multiply_divide_fusion
  640.9 299.2 %reduce-scatter.2.cloned.1.call-done = f32[64,512]{1,0:T(8,128)} async-done(((f32[4096,512]{1,0:T(8,128)}), f32[64,512]{1,0:T(8,128)}) %reduce-scatter.2.cloned.1.call-update) | async-done | bytes 131088 | tf_op jit(solution)/shard_map/reduce_scatter | solution.py:41
  940.1 0.0 copy-done.4
  940.1 1.6 divide_convert_fusion.4
Async XLA Ops:
  7.2 139.6 %all-reduce.4.cloned.1.call-start = ((), (), s32[]{:S(2)}) async-start(), calls=%async_computation.2 | async-start | bytes 2097152 | tf_op jit(solution)/shard_map/psum | solution.py:34
  8.6 61.2 %copy-start.1 = (f32[512,512]{1,0:T(8,128)S(1)}, f32[512,512]{1,0:T(8,128)}, u32[]{:S(2)}) copy-start(f32[512,512]{1,0:T(8,128)} %param.7) | copy-start | bytes 3145732
  69.8 12.0 %copy-start = (f32[512,64]{0,1:T(8,128)S(1)}, f32[512,64]{0,1:T(8,128)}, u32[]{:S(2)}) copy-start(f32[512,64]{0,1:T(8,128)} %param.8) | copy-start | bytes 393220
  81.3 65.4 %copy-start.5 = (f32[64,512]{1,0:T(8,128)S(1)}, f32[64,512]{1,0:T(8,128)}, u32[]{:S(2)}) copy-start(f32[64,512]{1,0:T(8,128)} %param.9) | copy-start | bytes 393220
  81.4 557.9 %all-reduce.6.cloned.1.call-start = ((), (), s32[]{:S(2)}) async-start(), calls=%async_computation.4 | async-start | bytes 262144 | tf_op jit(solution)/shard_map/psum | solution.py:51
  146.8 3.7 copy-start.2
  150.5 3.2 copy-start.3
  153.2 786.9 %reduce-scatter.2.cloned.1.call-start = ((), (), s32[]{:S(2)}) async-start(), calls=%async_computation.3 | async-start | bytes 8519680 | tf_op jit(solution)/shard_map/reduce_scatter | solution.py:41
  166.2 774.0 %copy-start.4 = (bf16[64,512]{1,0:T(8,128)(2,1)S(1)}, bf16[64,512]{1,0:T(8,128)(2,1)}, u32[]{:S(2)}) copy-start(bf16[64,512]{1,0:T(8,128)(2,1)} %param.6) | copy-start | bytes 196612
Sparse Core Ops, SparseCore 0:
  81.5 65.2 all-reduce.3
  153.3 485.9 all-reduce.5
  641.8 298.2 reduce-scatter.1
